TPU v7x, 128 devices: a whole 4x4x4 slice. The times are simulated.
128 devices in a mesh: dom: 16 (over z, y_hi, core), repl: 8 (over y_lo, x).
Axes of the slice: x: 4, y: 4 (y_hi: 2, y_lo: 2; y = y_hi * 2 + y_lo), z: 4, core: 2. Of those that a mesh axis runs over, the one named last changes fastest.
Arguments:
- features: bfloat16 [32768, 512], P(('dom', 'repl')), may hold values from -6 to 6
- cotangent: bfloat16 [32768, 512], P(('dom', 'repl')), may hold values from -6 to 6
- weight: bfloat16 [512, 512], replicated, may hold values from -0.25 to 0.25
- tiles: bfloat16 [16, 8, 16, 16, 128, 128], P('dom', 'repl'), may hold values from -0.0625 to 0.0625
- tile_rows: int32 [16, 8, 16, 16], P('dom', 'repl'), may hold values from 0 to 15
- tile_cols: int32 [16, 8, 16, 16], P('dom', 'repl'), may hold values from 0 to 1
- tile_counts: int32 [16, 8, 16], P('dom', 'repl'), may hold values from 1 to 16, as said below
Outputs:
- activated: bfloat16 [32768, 512], P(('dom', 'repl'))
- feature_grad: bfloat16 [32768, 512], P(('dom', 'repl'))
- weight_grad: float32 [512, 512], replicated
Inputs may be any that keep to these rules, and one draw needn't show every extreme that they name: `tile_counts`: live tiles of each row block, column group and column block; some entry equals 16 in every draw.
All inputs are finite; a program needn't handle non-finite values.
Results may differ from a plain program's by a relative error of at most 0.006.
Values may be sent and summed in bfloat16 or wider, within the bound.
A program may use at most 64 MiB of HBM per device.

v0:
```python
import jax
import jax.numpy as jnp
from jax import lax
from jax.sharding import PartitionSpec as P


def shifted(x, axis, by):
    length = lax.axis_size(axis)
    return lax.ppermute(x, axis, [(i, (i + by) % length) for i in range(length)])


def silu_slope(preact):
    sigma = jax.nn.sigmoid(preact)
    return sigma * (1.0 + preact * (1.0 - sigma))


def place_tiles(indices, prod, count):
    selector = (jnp.arange(count, dtype=jnp.int32)[:, None] == indices[None, :]).astype(jnp.float32)
    return jnp.einsum("rt,taf->raf", selector, prod, precision=lax.Precision.HIGHEST)


def local(features, cotangent, weight, tiles, tile_rows, tile_cols, tile_counts):
    blocks_count = lax.axis_size("dom")
    group_count = lax.axis_size("repl")
    rows_local, width = features.shape
    tile_size = tiles.shape[-1]
    slot_count = tiles.shape[3]
    col_tiles = rows_local // tile_size
    row_tiles = group_count * col_tiles
    slabs = tiles[0, 0]
    row_index = tile_rows[0, 0]
    col_index = tile_cols[0, 0]
    live_counts = tile_counts[0, 0]
    position = lax.axis_index("dom")
    scale = float(rows_local * blocks_count * group_count) ** (-0.5)

    def live_slab(column):
        slab_one = lax.dynamic_index_in_dim(slabs, column, 0, keepdims=False)
        alive = (jnp.arange(slot_count) < live_counts[column]).astype(jnp.bfloat16)
        return slab_one * alive[:, None, None]

    def forward_add(totals, source, column):
        slab_one = live_slab(column)
        picked = source.reshape(col_tiles, tile_size, width)[col_index[column]]
        prod = jnp.einsum("tab,tbf->taf", slab_one, picked, preferred_element_type=jnp.float32)
        return totals + place_tiles(row_index[column], prod, row_tiles)

    totals = forward_add(jnp.zeros((row_tiles, tile_size, width), jnp.float32), features, position)

    def forward_section(section, carry):
        sums, source = carry
        source = shifted(source, "dom", 1)
        return (forward_add(sums, source, (position - section) % blocks_count), source)

    totals, _ = lax.fori_loop(1, blocks_count, forward_section, (totals, features))
    totals = totals.reshape(row_tiles * tile_size, width)
    own_rows = lax.psum_scatter(totals, "repl", scatter_dimension=0, tiled=True)
    agg_rounded = own_rows.astype(jnp.bfloat16)
    preact = jnp.dot(agg_rounded, weight, preferred_element_type=jnp.float32)
    activated = jax.nn.silu(preact).astype(jnp.bfloat16)
    pre_grad = (cotangent.astype(jnp.float32) * silu_slope(preact)).astype(jnp.bfloat16)
    weight_part = lax.dot_general(
        agg_rounded, pre_grad, (((0,), (0,)), ((), ())), preferred_element_type=jnp.float32
    )
    weight_grad = lax.psum(weight_part, ("dom", "repl")) * scale
    agg_grad = lax.dot_general(
        pre_grad, weight, (((1,), (1,)), ((), ())), preferred_element_type=jnp.float32
    ).astype(jnp.bfloat16)
    block_grad = lax.all_gather(agg_grad, "repl", axis=0, tiled=True)
    grad_tiles = block_grad.reshape(row_tiles, tile_size, width)

    def backward_block(column):
        slab_one = live_slab(column)
        picked = grad_tiles[row_index[column]]
        prod = jnp.einsum("tab,taf->tbf", slab_one, picked, preferred_element_type=jnp.float32)
        return place_tiles(col_index[column], prod, col_tiles).reshape(rows_local, width)

    partial_value = backward_block((position - 1) % blocks_count)

    def backward_section(section, running):
        arrived = shifted(running, "dom", 1)
        return arrived + backward_block((position - section - 1) % blocks_count)

    summed = lax.fori_loop(1, blocks_count, backward_section, partial_value)
    feature_grad = summed.astype(jnp.bfloat16)
    return (activated, feature_grad, weight_grad)


def solution(mesh):
    in_specs = (
        P(("dom", "repl"), None),
        P(("dom", "repl"), None),
        P(),
        P("dom", "repl", None, None, None, None),
        P("dom", "repl", None, None),
        P("dom", "repl", None, None),
        P("dom", "repl", None),
    )
    out_specs = (P(("dom", "repl"), None), P(("dom", "repl"), None), P())
    return jax.shard_map(local, mesh=mesh, in_specs=in_specs, out_specs=out_specs, check_vma=False)
```

profile of v0, /device:TPU:0, one launch (start us, length us, event | category | flops | bytes accessed | tf_op | source)
XLA Modules:
  0.0 797.7 jit_solution(15760562931626630338)
XLA Ops:
  14.1 6.5 fusion.30
  20.6 309.1 %while.32 = (s32[]{:T(128)}, f32[16,128,512]{2,0,1:T(8,128)}, bf16[256,512]{1,0:T(8,128)(2,1)S(1)}, s32[]{:T(128)}, s32[16,16]{1,0:T(8,128)}, /*index=5*/bf16[16...) while((s32[]{:T(128)}, f32[16,128,512]{2,0,1:T(8,128)}, ...), condition=%wide.region_1.2_spmd, body=%wide.region_0.1_spmd.sunk | while | flops 471074144 | bytes 58725252 | solution.py:55
  23.2 7.6 collective-permute-done
  33.9 6.1 fusion.83
  44.6 6.8 collective-permute-done
  54.4 6.1 fusion.83
  65.2 6.8 collective-permute-done
  75.0 6.1 fusion.83
  85.7 6.8 collective-permute-done
  95.5 6.1 fusion.83
  106.3 6.8 collective-permute-done
  116.1 6.1 fusion.83
  126.8 6.8 collective-permute-done
  136.6 6.1 fusion.83
  147.4 6.8 collective-permute-done
  157.2 6.1 fusion.83
  167.9 6.8 collective-permute-done
  177.7 6.1 fusion.83
  188.5 6.8 collective-permute-done
  198.3 6.1 fusion.83
  209.0 6.8 collective-permute-done
  218.8 6.1 fusion.83
  229.6 6.8 collective-permute-done
  239.4 6.1 fusion.83
  250.1 6.8 collective-permute-done
  259.9 6.1 fusion.83
  270.7 6.8 collective-permute-done
  280.5 6.1 fusion.83
  291.2 6.8 collective-permute-done
  301.0 6.1 fusion.83
  311.8 6.8 collective-permute-done
  321.6 6.1 fusion.83
  329.7 6.6 copy.11
  336.3 49.7 %reduce-scatter.2.cloned.1.call-done = f32[256,512]{1,0:T(8,128)} async-done(((f32[2048,512]{1,0:T(8,128)}), f32[256,512]{1,0:T(8,128)}) %reduce-scatter.2.cloned.1.call-update) | async-done | bytes 524304 | tf_op jit(solution)/shard_map/reduce_scatter | solution.py:57
  388.2 2.5 fusion.38
  394.1 143.7 %all-reduce.2.cloned.1.call-done = f32[512,512]{1,0:T(8,128)} async-done(((f32[512,512]{1,0:T(8,128)}), f32[512,512]{1,0:T(8,128)}) %all-reduce.2.cloned.1.call-update) | async-done | bytes 1048592 | tf_op jit(solution)/shard_map/psum | solution.py:65
  537.8 2.3 broadcast_multiply_fusion
  540.1 40.4 %all-gather.2.cloned.1.call-done = bf16[2048,512]{1,0:T(8,128)(2,1)} async-done(((bf16[256,512]{1,0:T(8,128)(2,1)}), bf16[2048,512]{1,0:T(8,128)(2,1)}) %all-gather.2.cloned.1.call-update) | async-done | bytes 2097168 | tf_op jit(solution)/shard_map/all_gather | solution.py:69
  584.8 3.9 fusion.28
  589.6 199.8 %while.33 = (s32[]{:T(128)}, f32[256,512]{1,0:T(8,128)}, s32[]{:T(128)}, s32[16,16]{1,0:T(8,128)}, bf16[16,16,128,128]{3,2,1,0:T(8,128)(2,1)}, /*index=5*/s32[16...) while((s32[]{:T(128)}, f32[256,512]{1,0:T(8,128)}, ...), condition=%wide.region_4.5_spmd, body=%wide.region_3.4_spmd.sunk | while | flops 293995648 | bytes 20452200 | solution.py:84
  591.5 2.3 gather_fusion.1
  596.4 3.9 fusion.90
  606.1 2.3 gather_fusion.1
  611.0 3.9 fusion.90
  618.1 2.3 gather_fusion.1
  623.1 3.9 fusion.90
  631.6 2.3 gather_fusion.1
  636.5 3.9 fusion.90
  644.8 2.3 gather_fusion.1
  649.7 3.9 fusion.90
  658.1 2.3 gather_fusion.1
  663.1 3.9 fusion.90
  676.4 3.9 fusion.90
  689.7 3.9 fusion.90
  698.1 2.3 gather_fusion.1
  703.0 3.9 fusion.90
  716.3 3.9 fusion.90
  729.7 3.9 fusion.90
  738.0 2.3 gather_fusion.1
  743.0 3.9 fusion.90
  756.3 3.9 fusion.90
  769.6 3.9 fusion.90
  778.0 2.3 gather_fusion.1
  782.9 3.9 fusion.90
  (381 shorter events, 254.4 us)
Async XLA Ops:
  7.2 378.9 %copy-start = (bf16[512,512]{1,0:T(8,128)(2,1)S(1)}, bf16[512,512]{1,0:T(8,128)(2,1)}, u32[]{:S(2)}) copy-start(bf16[512,512]{1,0:T(8,128)(2,1)} %param.13) | copy-start | bytes 1572868
  7.2 378.9 %reduce-scatter.2.cloned.1.call-start = ((), (), s32[]{:S(2)}) async-start(), calls=%async_computation.1 | async-start | bytes 4718592 | tf_op jit(solution)/shard_map/reduce_scatter | solution.py:57
  14.1 6.5 copy-start.3
  20.6 10.3 %collective-permute-start = (bf16[256,512]{1,0:T(8,128)(2,1)S(1)}, bf16[256,512]{1,0:T(8,128)(2,1)S(1)}, u32[]{:S(2)}, u32[]{:S(2)}) collective-permute-start(bf16[256,512]{1,0:T(8,128)(2,1)S(1)} %get-tuple-element.552), channel_id=1, source_target_pairs={{0,8},{8,16},{16,24},{24,32},{32,40},{40,48},{48,56},{56,64},{64,7... | collective-permute-start | bytes 786440 | tf_op jit(solution)/shard_map/while/body/eval_jaxpr/ppermute | solution.py:9
  31.5 2.3 copy-start.1
  40.0 2.0 copy-start.2
  42.0 9.4 %collective-permute-start = (bf16[256,512]{1,0:T(8,128)(2,1)S(1)}, bf16[256,512]{1,0:T(8,128)(2,1)S(1)}, u32[]{:S(2)}, u32[]{:S(2)}) collective-permute-start(bf16[256,512]{1,0:T(8,128)(2,1)S(1)} %get-tuple-element.552), channel_id=1, source_target_pairs={{0,8},{8,16},{16,24},{24,32},{32,40},{40,48},{48,56},{56,64},{64,7... | collective-permute-start | bytes 786440 | tf_op jit(solution)/shard_map/while/body/eval_jaxpr/ppermute | solution.py:9
  52.1 2.3 copy-start.1
  60.6 2.0 copy-start.2
  62.5 9.4 %collective-permute-start = (bf16[256,512]{1,0:T(8,128)(2,1)S(1)}, bf16[256,512]{1,0:T(8,128)(2,1)S(1)}, u32[]{:S(2)}, u32[]{:S(2)}) collective-permute-start(bf16[256,512]{1,0:T(8,128)(2,1)S(1)} %get-tuple-element.552), channel_id=1, source_target_pairs={{0,8},{8,16},{16,24},{24,32},{32,40},{40,48},{48,56},{56,64},{64,7... | collective-permute-start | bytes 786440 | tf_op jit(solution)/shard_map/while/body/eval_jaxpr/ppermute | solution.py:9
  72.6 2.3 copy-start.1
  81.1 2.0 copy-start.2
  83.1 9.4 %collective-permute-start = (bf16[256,512]{1,0:T(8,128)(2,1)S(1)}, bf16[256,512]{1,0:T(8,128)(2,1)S(1)}, u32[]{:S(2)}, u32[]{:S(2)}) collective-permute-start(bf16[256,512]{1,0:T(8,128)(2,1)S(1)} %get-tuple-element.552), channel_id=1, source_target_pairs={{0,8},{8,16},{16,24},{24,32},{32,40},{40,48},{48,56},{56,64},{64,7... | collective-permute-start | bytes 786440 | tf_op jit(solution)/shard_map/while/body/eval_jaxpr/ppermute | solution.py:9
  93.2 2.3 copy-start.1
  101.7 2.0 copy-start.2
  103.6 9.4 %collective-permute-start = (bf16[256,512]{1,0:T(8,128)(2,1)S(1)}, bf16[256,512]{1,0:T(8,128)(2,1)S(1)}, u32[]{:S(2)}, u32[]{:S(2)}) collective-permute-start(bf16[256,512]{1,0:T(8,128)(2,1)S(1)} %get-tuple-element.552), channel_id=1, source_target_pairs={{0,8},{8,16},{16,24},{24,32},{32,40},{40,48},{48,56},{56,64},{64,7... | collective-permute-start | bytes 786440 | tf_op jit(solution)/shard_map/while/body/eval_jaxpr/ppermute | solution.py:9
  113.7 2.3 copy-start.1
  122.2 2.0 copy-start.2
  124.2 9.4 %collective-permute-start = (bf16[256,512]{1,0:T(8,128)(2,1)S(1)}, bf16[256,512]{1,0:T(8,128)(2,1)S(1)}, u32[]{:S(2)}, u32[]{:S(2)}) collective-permute-start(bf16[256,512]{1,0:T(8,128)(2,1)S(1)} %get-tuple-element.552), channel_id=1, source_target_pairs={{0,8},{8,16},{16,24},{24,32},{32,40},{40,48},{48,56},{56,64},{64,7... | collective-permute-start | bytes 786440 | tf_op jit(solution)/shard_map/while/body/eval_jaxpr/ppermute | solution.py:9
  134.3 2.3 copy-start.1
  142.8 2.0 copy-start.2
  144.7 9.4 %collective-permute-start = (bf16[256,512]{1,0:T(8,128)(2,1)S(1)}, bf16[256,512]{1,0:T(8,128)(2,1)S(1)}, u32[]{:S(2)}, u32[]{:S(2)}) collective-permute-start(bf16[256,512]{1,0:T(8,128)(2,1)S(1)} %get-tuple-element.552), channel_id=1, source_target_pairs={{0,8},{8,16},{16,24},{24,32},{32,40},{40,48},{48,56},{56,64},{64,7... | collective-permute-start | bytes 786440 | tf_op jit(solution)/shard_map/while/body/eval_jaxpr/ppermute | solution.py:9
  154.8 2.3 copy-start.1
  163.3 2.0 copy-start.2
  165.3 9.4 %collective-permute-start = (bf16[256,512]{1,0:T(8,128)(2,1)S(1)}, bf16[256,512]{1,0:T(8,128)(2,1)S(1)}, u32[]{:S(2)}, u32[]{:S(2)}) collective-permute-start(bf16[256,512]{1,0:T(8,128)(2,1)S(1)} %get-tuple-element.552), channel_id=1, source_target_pairs={{0,8},{8,16},{16,24},{24,32},{32,40},{40,48},{48,56},{56,64},{64,7... | collective-permute-start | bytes 786440 | tf_op jit(solution)/shard_map/while/body/eval_jaxpr/ppermute | solution.py:9
  175.4 2.3 copy-start.1
  183.9 2.0 copy-start.2
  185.9 9.4 %collective-permute-start = (bf16[256,512]{1,0:T(8,128)(2,1)S(1)}, bf16[256,512]{1,0:T(8,128)(2,1)S(1)}, u32[]{:S(2)}, u32[]{:S(2)}) collective-permute-start(bf16[256,512]{1,0:T(8,128)(2,1)S(1)} %get-tuple-element.552), channel_id=1, source_target_pairs={{0,8},{8,16},{16,24},{24,32},{32,40},{40,48},{48,56},{56,64},{64,7... | collective-permute-start | bytes 786440 | tf_op jit(solution)/shard_map/while/body/eval_jaxpr/ppermute | solution.py:9
  195.9 2.3 copy-start.1
  204.4 2.0 copy-start.2
  206.4 9.4 %collective-permute-start = (bf16[256,512]{1,0:T(8,128)(2,1)S(1)}, bf16[256,512]{1,0:T(8,128)(2,1)S(1)}, u32[]{:S(2)}, u32[]{:S(2)}) collective-permute-start(bf16[256,512]{1,0:T(8,128)(2,1)S(1)} %get-tuple-element.552), channel_id=1, source_target_pairs={{0,8},{8,16},{16,24},{24,32},{32,40},{40,48},{48,56},{56,64},{64,7... | collective-permute-start | bytes 786440 | tf_op jit(solution)/shard_map/while/body/eval_jaxpr/ppermute | solution.py:9
  216.5 2.3 copy-start.1
  225.0 2.0 copy-start.2
  227.0 9.4 %collective-permute-start = (bf16[256,512]{1,0:T(8,128)(2,1)S(1)}, bf16[256,512]{1,0:T(8,128)(2,1)S(1)}, u32[]{:S(2)}, u32[]{:S(2)}) collective-permute-start(bf16[256,512]{1,0:T(8,128)(2,1)S(1)} %get-tuple-element.552), channel_id=1, source_target_pairs={{0,8},{8,16},{16,24},{24,32},{32,40},{40,48},{48,56},{56,64},{64,7... | collective-permute-start | bytes 786440 | tf_op jit(solution)/shard_map/while/body/eval_jaxpr/ppermute | solution.py:9
  237.1 2.3 copy-start.1
  245.5 2.0 copy-start.2
  247.5 9.4 %collective-permute-start = (bf16[256,512]{1,0:T(8,128)(2,1)S(1)}, bf16[256,512]{1,0:T(8,128)(2,1)S(1)}, u32[]{:S(2)}, u32[]{:S(2)}) collective-permute-start(bf16[256,512]{1,0:T(8,128)(2,1)S(1)} %get-tuple-element.552), channel_id=1, source_target_pairs={{0,8},{8,16},{16,24},{24,32},{32,40},{40,48},{48,56},{56,64},{64,7... | collective-permute-start | bytes 786440 | tf_op jit(solution)/shard_map/while/body/eval_jaxpr/ppermute | solution.py:9
  257.6 2.3 copy-start.1
  266.1 2.0 copy-start.2
  268.1 9.4 %collective-permute-start = (bf16[256,512]{1,0:T(8,128)(2,1)S(1)}, bf16[256,512]{1,0:T(8,128)(2,1)S(1)}, u32[]{:S(2)}, u32[]{:S(2)}) collective-permute-start(bf16[256,512]{1,0:T(8,128)(2,1)S(1)} %get-tuple-element.552), channel_id=1, source_target_pairs={{0,8},{8,16},{16,24},{24,32},{32,40},{40,48},{48,56},{56,64},{64,7... | collective-permute-start | bytes 786440 | tf_op jit(solution)/shard_map/while/body/eval_jaxpr/ppermute | solution.py:9
  278.1 2.3 copy-start.1
  286.6 2.0 copy-start.2
  288.6 9.4 %collective-permute-start = (bf16[256,512]{1,0:T(8,128)(2,1)S(1)}, bf16[256,512]{1,0:T(8,128)(2,1)S(1)}, u32[]{:S(2)}, u32[]{:S(2)}) collective-permute-start(bf16[256,512]{1,0:T(8,128)(2,1)S(1)} %get-tuple-element.552), channel_id=1, source_target_pairs={{0,8},{8,16},{16,24},{24,32},{32,40},{40,48},{48,56},{56,64},{64,7... | collective-permute-start | bytes 786440 | tf_op jit(solution)/shard_map/while/body/eval_jaxpr/ppermute | solution.py:9
  298.7 2.3 copy-start.1
  309.2 9.4 %collective-permute-start = (bf16[256,512]{1,0:T(8,128)(2,1)S(1)}, bf16[256,512]{1,0:T(8,128)(2,1)S(1)}, u32[]{:S(2)}, u32[]{:S(2)}) collective-permute-start(bf16[256,512]{1,0:T(8,128)(2,1)S(1)} %get-tuple-element.552), channel_id=1, source_target_pairs={{0,8},{8,16},{16,24},{24,32},{32,40},{40,48},{48,56},{56,64},{64,7... | collective-permute-start | bytes 786440 | tf_op jit(solution)/shard_map/while/body/eval_jaxpr/ppermute | solution.py:9
  319.3 2.3 copy-start.1
  336.3 51.9 %copy-start.4 = (bf16[256,512]{1,0:T(8,128)(2,1)S(1)}, bf16[256,512]{1,0:T(8,128)(2,1)}, u32[]{:S(2)}) copy-start(bf16[256,512]{1,0:T(8,128)(2,1)} %param.12) | copy-start | bytes 786436
  336.3 201.5 %all-reduce.2.cloned.1.call-start = ((), (), s32[]{:S(2)}) async-start(), calls=%async_computation.3 | async-start | bytes 2097152 | tf_op jit(solution)/shard_map/psum | solution.py:65
  390.7 189.9 %all-gather.2.cloned.1.call-start = ((), (), s32[]{:S(2)}) async-start(), calls=%async_computation.2 | async-start | bytes 2359296 | tf_op jit(solution)/shard_map/all_gather | solution.py:69
  589.6 12.4 %collective-permute-start.1 = (f32[256,512]{1,0:T(8,128)}, f32[256,512]{1,0:T(8,128)S(1)}, u32[]{:S(2)}, u32[]{:S(2)}) collective-permute-start(f32[256,512]{1,0:T(8,128)} %get-tuple-element.588), channel_id=1, source_target_pairs={{0,8},{8,16},{16,24},{24,32},{32,40},{40,48},{48,56},{56,64},{64,7... | collective-permute-start | bytes 1572872 | tf_op jit(solution)/shard_map/while/body/eval_jaxpr/ppermute | solution.py:9
  602.9 12.4 %collective-permute-start.1 = (f32[256,512]{1,0:T(8,128)}, f32[256,512]{1,0:T(8,128)S(1)}, u32[]{:S(2)}, u32[]{:S(2)}) collective-permute-start(f32[256,512]{1,0:T(8,128)} %get-tuple-element.588), channel_id=1, source_target_pairs={{0,8},{8,16},{16,24},{24,32},{32,40},{40,48},{48,56},{56,64},{64,7... | collective-permute-start | bytes 1572872 | tf_op jit(solution)/shard_map/while/body/eval_jaxpr/ppermute | solution.py:9
  616.2 12.4 %collective-permute-start.1 = (f32[256,512]{1,0:T(8,128)}, f32[256,512]{1,0:T(8,128)S(1)}, u32[]{:S(2)}, u32[]{:S(2)}) collective-permute-start(f32[256,512]{1,0:T(8,128)} %get-tuple-element.588), channel_id=1, source_target_pairs={{0,8},{8,16},{16,24},{24,32},{32,40},{40,48},{48,56},{56,64},{64,7... | collective-permute-start | bytes 1572872 | tf_op jit(solution)/shard_map/while/body/eval_jaxpr/ppermute | solution.py:9
  629.5 12.4 %collective-permute-start.1 = (f32[256,512]{1,0:T(8,128)}, f32[256,512]{1,0:T(8,128)S(1)}, u32[]{:S(2)}, u32[]{:S(2)}) collective-permute-start(f32[256,512]{1,0:T(8,128)} %get-tuple-element.588), channel_id=1, source_target_pairs={{0,8},{8,16},{16,24},{24,32},{32,40},{40,48},{48,56},{56,64},{64,7... | collective-permute-start | bytes 1572872 | tf_op jit(solution)/shard_map/while/body/eval_jaxpr/ppermute | solution.py:9
  642.8 12.4 %collective-permute-start.1 = (f32[256,512]{1,0:T(8,128)}, f32[256,512]{1,0:T(8,128)S(1)}, u32[]{:S(2)}, u32[]{:S(2)}) collective-permute-start(f32[256,512]{1,0:T(8,128)} %get-tuple-element.588), channel_id=1, source_target_pairs={{0,8},{8,16},{16,24},{24,32},{32,40},{40,48},{48,56},{56,64},{64,7... | collective-permute-start | bytes 1572872 | tf_op jit(solution)/shard_map/while/body/eval_jaxpr/ppermute | solution.py:9
  656.2 12.4 %collective-permute-start.1 = (f32[256,512]{1,0:T(8,128)}, f32[256,512]{1,0:T(8,128)S(1)}, u32[]{:S(2)}, u32[]{:S(2)}) collective-permute-start(f32[256,512]{1,0:T(8,128)} %get-tuple-element.588), channel_id=1, source_target_pairs={{0,8},{8,16},{16,24},{24,32},{32,40},{40,48},{48,56},{56,64},{64,7... | collective-permute-start | bytes 1572872 | tf_op jit(solution)/shard_map/while/body/eval_jaxpr/ppermute | solution.py:9
  669.5 12.4 %collective-permute-start.1 = (f32[256,512]{1,0:T(8,128)}, f32[256,512]{1,0:T(8,128)S(1)}, u32[]{:S(2)}, u32[]{:S(2)}) collective-permute-start(f32[256,512]{1,0:T(8,128)} %get-tuple-element.588), channel_id=1, source_target_pairs={{0,8},{8,16},{16,24},{24,32},{32,40},{40,48},{48,56},{56,64},{64,7... | collective-permute-start | bytes 1572872 | tf_op jit(solution)/shard_map/while/body/eval_jaxpr/ppermute | solution.py:9
  682.8 12.4 %collective-permute-start.1 = (f32[256,512]{1,0:T(8,128)}, f32[256,512]{1,0:T(8,128)S(1)}, u32[]{:S(2)}, u32[]{:S(2)}) collective-permute-start(f32[256,512]{1,0:T(8,128)} %get-tuple-element.588), channel_id=1, source_target_pairs={{0,8},{8,16},{16,24},{24,32},{32,40},{40,48},{48,56},{56,64},{64,7... | collective-permute-start | bytes 1572872 | tf_op jit(solution)/shard_map/while/body/eval_jaxpr/ppermute | solution.py:9
  696.1 12.4 %collective-permute-start.1 = (f32[256,512]{1,0:T(8,128)}, f32[256,512]{1,0:T(8,128)S(1)}, u32[]{:S(2)}, u32[]{:S(2)}) collective-permute-start(f32[256,512]{1,0:T(8,128)} %get-tuple-element.588), channel_id=1, source_target_pairs={{0,8},{8,16},{16,24},{24,32},{32,40},{40,48},{48,56},{56,64},{64,7... | collective-permute-start | bytes 1572872 | tf_op jit(solution)/shard_map/while/body/eval_jaxpr/ppermute | solution.py:9
  709.4 12.4 %collective-permute-start.1 = (f32[256,512]{1,0:T(8,128)}, f32[256,512]{1,0:T(8,128)S(1)}, u32[]{:S(2)}, u32[]{:S(2)}) collective-permute-start(f32[256,512]{1,0:T(8,128)} %get-tuple-element.588), channel_id=1, source_target_pairs={{0,8},{8,16},{16,24},{24,32},{32,40},{40,48},{48,56},{56,64},{64,7... | collective-permute-start | bytes 1572872 | tf_op jit(solution)/shard_map/while/body/eval_jaxpr/ppermute | solution.py:9
  722.8 12.4 %collective-permute-start.1 = (f32[256,512]{1,0:T(8,128)}, f32[256,512]{1,0:T(8,128)S(1)}, u32[]{:S(2)}, u32[]{:S(2)}) collective-permute-start(f32[256,512]{1,0:T(8,128)} %get-tuple-element.588), channel_id=1, source_target_pairs={{0,8},{8,16},{16,24},{24,32},{32,40},{40,48},{48,56},{56,64},{64,7... | collective-permute-start | bytes 1572872 | tf_op jit(solution)/shard_map/while/body/eval_jaxpr/ppermute | solution.py:9
  736.1 12.4 %collective-permute-start.1 = (f32[256,512]{1,0:T(8,128)}, f32[256,512]{1,0:T(8,128)S(1)}, u32[]{:S(2)}, u32[]{:S(2)}) collective-permute-start(f32[256,512]{1,0:T(8,128)} %get-tuple-element.588), channel_id=1, source_target_pairs={{0,8},{8,16},{16,24},{24,32},{32,40},{40,48},{48,56},{56,64},{64,7... | collective-permute-start | bytes 1572872 | tf_op jit(solution)/shard_map/while/body/eval_jaxpr/ppermute | solution.py:9
  749.4 12.4 %collective-permute-start.1 = (f32[256,512]{1,0:T(8,128)}, f32[256,512]{1,0:T(8,128)S(1)}, u32[]{:S(2)}, u32[]{:S(2)}) collective-permute-start(f32[256,512]{1,0:T(8,128)} %get-tuple-element.588), channel_id=1, source_target_pairs={{0,8},{8,16},{16,24},{24,32},{32,40},{40,48},{48,56},{56,64},{64,7... | collective-permute-start | bytes 1572872 | tf_op jit(solution)/shard_map/while/body/eval_jaxpr/ppermute | solution.py:9
  762.7 12.4 %collective-permute-start.1 = (f32[256,512]{1,0:T(8,128)}, f32[256,512]{1,0:T(8,128)S(1)}, u32[]{:S(2)}, u32[]{:S(2)}) collective-permute-start(f32[256,512]{1,0:T(8,128)} %get-tuple-element.588), channel_id=1, source_target_pairs={{0,8},{8,16},{16,24},{24,32},{32,40},{40,48},{48,56},{56,64},{64,7... | collective-permute-start | bytes 1572872 | tf_op jit(solution)/shard_map/while/body/eval_jaxpr/ppermute | solution.py:9
  776.0 12.4 %collective-permute-start.1 = (f32[256,512]{1,0:T(8,128)}, f32[256,512]{1,0:T(8,128)S(1)}, u32[]{:S(2)}, u32[]{:S(2)}) collective-permute-start(f32[256,512]{1,0:T(8,128)} %get-tuple-element.588), channel_id=1, source_target_pairs={{0,8},{8,16},{16,24},{24,32},{32,40},{40,48},{48,56},{56,64},{64,7... | collective-permute-start | bytes 1572872 | tf_op jit(solution)/shard_map/while/body/eval_jaxpr/ppermute | solution.py:9
  (2 other events, 3.9 us)
Sparse Core Ops, SparseCore 0:
  336.4 49.5 reduce-scatter.1
  391.4 146.3 all-reduce.1
  540.1 40.4 all-gather.1
where the time goes:
time: 802 us; the launch traced here: 798 us
  waiting for transfers between devices  358 us (45%)
  matrix products  228 us (28%)
  local copies, waits for them, and re-layouts  134 us (17%)
  other arithmetic  60.5 us (8%)
  between operations  13.8 us (2%)
    dot_general x32, matrix products, place_tiles(): jnp.einsum('rt,taf->raf', selector, prod, precision=lax.Precision.HIGHEST)  160 us
    psum x1, waiting for transfers between devices, local(): weight_grad = lax.psum(weight_part, ('dom', 'repl')) * scale  144 us
    ppermute x30, waiting for transfers between devices, shifted(): lax.ppermute(x, axis, [(i, (i + by) % length) for i in range(length)])  125 us
    reduce_scatter x1, waiting for transfers between devices, local(): own_rows = lax.psum_scatter(totals, 'repl', scatter_dimension=0, tiled=True)  49.7 us
    all_gather x1, waiting for transfers between devices, local(): block_grad = lax.all_gather(agg_grad, 'repl', axis=0, tiled=True)  40.4 us
    gather x16, local copies, waits for them, and re-layouts, backward_block(): picked = grad_tiles[row_index[column]]  36.4 us
    while x75, local copies, waits for them, and re-layouts  35.2 us
    dot_general x16, matrix products, backward_block(): jnp.einsum('tab,taf->tbf', slab_one, picked, preferred_element_type=jnp.f...  31.5 us
  transfers between devices with their start and end apart: 33, of which 33 were waited for; matrix products, arithmetic and copies ran while one was open for 26% of the time, Pallas kernels for 0%

commit v1 on v0

v1 whole, which is shorter than its diff:
```python
import functools

import jax
import jax.numpy as jnp
from jax import lax
from jax.experimental import pallas as pl
from jax.experimental.pallas import tpu as pltpu
from jax.sharding import PartitionSpec as P

F32 = jnp.float32
BF16 = jnp.bfloat16
MESH = pl.DeviceIdType.MESH
Z, YH, CO, YL, X = 4, 2, 2, 2, 4
NDOM, NREP = Z * YH * CO, YL * X


class Names:
    def __init__(self):
        self.count = 0

    def take(self, n=1):
        base = self.count
        self.count += n
        return base


def message_table():
    names = Names()
    table = {}
    for h in (0, 1):
        for kind, n in (("zp", 2), ("zm", 2), ("y", 1), ("f", 2), ("sib", 8)):
            table["A", kind, h] = names.take(n)
        for kind, n in (("2p", 1), ("2m", 1), ("p", 1), ("m", 1), ("y", 1)):
            table["B", kind, h] = names.take(n)
        for kind, n in (("xp", 2), ("xm", 2), ("y", 1), ("f", 2)):
            table["D", kind, h] = names.take(n)
        for kind, n in (("sib", 8), ("2p", 1), ("2m", 1), ("p", 2), ("m", 2), ("y", 1)):
            table["E", kind, h] = names.take(n)
    for kind in ("rc", "gc"):
        table["W", kind] = names.take(1)
    for kind in ("rz", "ry", "rx", "gx", "gy", "gz"):
        table["W", kind] = names.take(3)
    return table, names.count


def kernel(dims, table, chain_ref, feat_ref, cot_ref, w_ref, tiles_ref,
           act_ref, fgrad_ref, wgrad_ref, *scratch):
    rows, width, tile, slots = dims
    half = width // 2
    scale = float(rows * NDOM * NREP) ** (-0.5)
    (tbuf, rbuf, adj, fbuf, gbuf, pacc, eacc, agg, preact,
     bs2, bsp, bsm, bsy, br2p, br2m, brp, brm, bry,
     ess, es2, esp, esm, esy, ers, er2p, er2m, erp, erm, ery,
     wpart, wrc, wzb, wrz, w2, wry, w3, wrx, wfull,
     tsem, fsem, ssem, rsem) = scratch

    dom = lax.axis_index("dom")
    rep = lax.axis_index("repl")
    co = lax.rem(dom, 2)
    yh = lax.rem(lax.div(dom, 2), 2)
    z = lax.div(dom, 4)
    x = lax.rem(rep, 4)
    yl = lax.div(rep, 4)
    y = yh * 2 + yl

    def turn(v, by):
        return lax.rem(v + by, 4)

    zu, zd, z2 = turn(z, 1), turn(z, 3), turn(z, 2)
    xu, xd, x2 = turn(x, 1), turn(x, 3), turn(x, 2)

    def did(z_, yh_, co_):
        return z_ * 4 + yh_ * 2 + co_

    def at_y(y_):
        return (did(z, lax.div(y_, 2), co), lax.rem(y_, 2) * 4 + x)

    dev_sib = (did(z, yh, 1 - co), rep)
    dev_zu, dev_zd = (did(zu, yh, co), rep), (did(zd, yh, co), rep)
    dev_yp = (did(z, 1 - yh, co), rep)
    dev_xu, dev_xd = (dom, yl * 4 + xu), (dom, yl * 4 + xd)
    dev_yl = (dom, (1 - yl) * 4 + x)
    zpeers = [(did(turn(z, k), yh, co), rep) for k in (1, 2, 3)]
    ypeers = [at_y(turn(y, k)) for k in (1, 2, 3)]
    xpeers = [(dom, yl * 4 + turn(x, k)) for k in (1, 2, 3)]

    pending = []

    def send(src, dst, number, dev, slot=None):
        arrival = number if slot is None else number + slot
        copy = pltpu.make_async_remote_copy(
            src_ref=src, dst_ref=dst, send_sem=ssem.at[len(pending)], recv_sem=rsem.at[arrival],
            device_id=dev, device_id_type=MESH)
        copy.start()
        pending.append(copy)

    def arrived(dst, number):
        pltpu.make_async_remote_copy(
            src_ref=dst, dst_ref=dst, send_sem=ssem.at[0], recv_sem=rsem.at[number],
            device_id=dev_sib, device_id_type=MESH).wait_recv()

    def slab(c):
        return pl.ds(pl.multiple_of(c * rows, rows), rows)

    for c in range(NDOM):
        pltpu.make_async_copy(tiles_ref.at[c], tbuf.at[c], tsem.at[c]).start()
    for h in (0, 1):
        pltpu.make_async_copy(
            feat_ref.at[:, h * half:(h + 1) * half], fbuf.at[h, slab(dom)], fsem.at[h]).start()
    barrier = pltpu.get_barrier_semaphore()
    partners = [dev_sib] + zpeers + ypeers + xpeers
    for dev in partners:
        pl.semaphore_signal(barrier, inc=1, device_id=dev, device_id_type=MESH)
    rbuf[slots] = jnp.zeros((tile, tile), F32)
    pl.semaphore_wait(barrier, len(partners))

    def a_slot(kind, core):
        return {
            "own": did(z, yh, core), "par": did(z, 1 - yh, core),
            "zp0": did(zd, 0, core), "zp1": did(zd, 1, core),
            "zm0": did(zu, 0, core), "zm1": did(zu, 1, core),
            "f0": did(z2, 0, core), "f1": did(z2, 1, core),
        }[kind]

    a_kinds = ("own", "par", "zp0", "zm1", "zp1", "zm0", "f0", "f1")

    def a_send(h, kind, number, dev, slot=None):
        block = fbuf.at[h, slab(a_slot(kind, co))]
        send(block, block, number, dev, slot)

    def a_sib(h, kind):
        a_send(h, kind, table["A", "sib", h] + a_kinds.index(kind), dev_sib)

    def a_wait(h, kind, number):
        arrived(fbuf.at[h, slab(a_slot(kind, co))], number)

    def a_own(h):
        pltpu.make_async_copy(
            feat_ref.at[:, h * half:(h + 1) * half], fbuf.at[h, slab(dom)], fsem.at[h]).wait()
        a_send(h, "own", table["A", "zp", h], dev_zu, yh)
        a_send(h, "own", table["A", "zm", h], dev_zd, yh)
        a_send(h, "own", table["A", "y", h], dev_yp)
        a_sib(h, "own")

    def a_par(h):
        a_wait(h, "par", table["A", "y", h])
        a_send(h, "par", table["A", "zp", h], dev_zu, 1 - yh)
        a_send(h, "par", table["A", "zm", h], dev_zd, 1 - yh)
        a_sib(h, "par")

    def a_ring(h):
        a_wait(h, "zp0", table["A", "zp", h])
        a_send(h, "zp0", table["A", "f", h], dev_zu)
        a_sib(h, "zp0")
        a_wait(h, "zm1", table["A", "zm", h] + 1)
        a_send(h, "zm1", table["A", "f", h] + 1, dev_zd)
        a_sib(h, "zm1")
        a_wait(h, "zp1", table["A", "zp", h] + 1)
        a_sib(h, "zp1")
        a_wait(h, "zm0", table["A", "zm", h])
        a_sib(h, "zm0")

    def a_far(h):
        for k in (0, 1):
            a_wait(h, f"f{k}", table["A", "f", h] + k)
            a_sib(h, f"f{k}")

    def a_end(h):
        for i, kind in enumerate(a_kinds):
            arrived(fbuf.at[h, slab(a_slot(kind, 1 - co))], table["A", "sib", h] + i)

    def densify(first, last):
        @pl.loop(first, last)
        def _(c):
            pltpu.make_async_copy(tiles_ref.at[c], tbuf.at[c], tsem.at[c]).wait()
            for t in range(slots):
                rbuf[t] = tbuf[c, t].astype(F32) + rbuf[chain_ref[c, t]]
            for p in range(4 * NREP):
                r, k = p // 2, p % 2
                g, i = r // 2, r % 2
                row = ((g % 4 * 2 + g // 4) * 2 + i) * tile
                lane = pl.multiple_of(c * rows + k * tile, tile)
                adj[row:row + tile, pl.ds(lane, tile)] = rbuf[chain_ref[c, slots + p]].astype(BF16)

    def rows_of(x_):
        return pl.ds(pl.multiple_of(x_ * 2 * rows, 2 * rows), 2 * rows)

    def b_part(h, slot, x_):
        @pl.loop(0, 2)
        def _(i):
            where = pl.multiple_of(x_ * 2 * rows + i * rows, rows)
            pacc[slot, i] = jnp.dot(adj[pl.ds(where, rows), :], fbuf[h], preferred_element_type=F32)

    def b_first(h):
        b_part(h, 0, x2)
        bs2[h] = pacc[0].astype(BF16)
        send(bs2.at[h, 0], br2p.at[h], table["B", "2p", h], dev_xu)
        send(bs2.at[h, 1], br2m.at[h], table["B", "2m", h], dev_xd)

    def b_second(h):
        arrived(br2p.at[h], table["B", "2p", h])
        bsp[h, 0] = (pacc[1, 0] + br2p[h].astype(F32)).astype(BF16)
        bsp[h, 1] = pacc[1, 1].astype(BF16)
        send(bsp.at[h], brp.at[h], table["B", "p", h], dev_xu)
        arrived(br2m.at[h], table["B", "2m", h])
        bsm[h, 0] = pacc[2, 0].astype(BF16)
        bsm[h, 1] = (pacc[2, 1] + br2m[h].astype(F32)).astype(BF16)
        send(bsm.at[h], brm.at[h], table["B", "m", h], dev_xd)

    def b_third(h):
        arrived(brp.at[h], table["B", "p", h])
        arrived(brm.at[h], table["B", "m", h])
        other = 1 - yl
        bsy[h] = (pacc[3, other] + brp[h, other].astype(F32) + brm[h, other].astype(F32)).astype(BF16)
        send(bsy.at[h], bry.at[h], table["B", "y", h], dev_yl)
        pacc[3, yl] = pacc[3, yl] + brp[h, yl].astype(F32) + brm[h, yl].astype(F32)

    def b_fourth(h):
        arrived(bry.at[h], table["B", "y", h])
        agg[:, h * half:(h + 1) * half] = (pacc[3, yl] + bry[h].astype(F32)).astype(BF16)

    def d_slot(kind):
        x_, yl_ = {
            "own": (x, yl), "par": (x, 1 - yl), "xp0": (xd, 0), "xp1": (xd, 1),
            "xm0": (xu, 0), "xm1": (xu, 1), "f0": (x2, 0), "f1": (x2, 1),
        }[kind]
        return pl.ds(pl.multiple_of((x_ * 2 + yl_) * rows, rows), rows)

    def d_send(h, kind, number, dev, slot=None):
        block = gbuf.at[h, :, d_slot(kind)]
        send(block, block, number, dev, slot)

    def d_wait(h, kind, number):
        arrived(gbuf.at[h, :, d_slot(kind)], number)

    def d_own(h):
        d_send(h, "own", table["D", "y", h], dev_yl)
        d_send(h, "own", table["D", "xp", h], dev_xu, yl)
        d_send(h, "own", table["D", "xm", h], dev_xd, yl)

    def d_par(h):
        d_wait(h, "par", table["D", "y", h])
        d_send(h, "par", table["D", "xp", h], dev_xu, 1 - yl)
        d_send(h, "par", table["D", "xm", h], dev_xd, 1 - yl)

    def d_ring(h):
        d_wait(h, "xp0", table["D", "xp", h])
        d_send(h, "xp0", table["D", "f", h], dev_xu)
        d_wait(h, "xm1", table["D", "xm", h] + 1)
        d_send(h, "xm1", table["D", "f", h] + 1, dev_xd)
        d_wait(h, "xp1", table["D", "xp", h] + 1)
        d_wait(h, "xm0", table["D", "xm", h])

    def d_far(h):
        for k in (0, 1):
            d_wait(h, f"f{k}", table["D", "f", h] + k)

    zs = (z2, zu, zd, z)

    def e_part(h, kind):
        @pl.loop(0, 2)
        def _(i):
            there = did(zs[kind], i, 1 - co)
            here = did(zs[kind], i, co)
            ess[h, kind, i] = jnp.dot(
                gbuf[h], adj[:, slab(there)], preferred_element_type=F32).astype(BF16)
            eacc[kind, i] = jnp.dot(gbuf[h], adj[:, slab(here)], preferred_element_type=F32)

        for i in (0, 1):
            send(ess.at[h, kind, i], ers.at[h, kind, i], table["E", "sib", h] + kind * 2 + i, dev_sib)

    def e_joined(h, kind, i):
        arrived(ers.at[h, kind, i], table["E", "sib", h] + kind * 2 + i)
        return eacc[kind, i] + ers[h, kind, i].astype(F32)

    def e_first(h):
        es2[h, 0] = e_joined(h, 0, 0).astype(BF16)
        send(es2.at[h, 0], er2p.at[h], table["E", "2p", h], dev_zu)
        es2[h, 1] = e_joined(h, 0, 1).astype(BF16)
        send(es2.at[h, 1], er2m.at[h], table["E", "2m", h], dev_zd)

    def e_second(h):
        esp[h, 1] = e_joined(h, 1, 1).astype(BF16)
        send(esp.at[h, 1], erp.at[h, 1], table["E", "p", h] + 1, dev_zu)
        esm[h, 0] = e_joined(h, 2, 0).astype(BF16)
        send(esm.at[h, 0], erm.at[h, 0], table["E", "m", h], dev_zd)
        value = e_joined(h, 1, 0)
        arrived(er2p.at[h], table["E", "2p", h])
        esp[h, 0] = (value + er2p[h].astype(F32)).astype(BF16)
        send(esp.at[h, 0], erp.at[h, 0], table["E", "p", h], dev_zu)
        value = e_joined(h, 2, 1)
        arrived(er2m.at[h], table["E", "2m", h])
        esm[h, 1] = (value + er2m[h].astype(F32)).astype(BF16)
        send(esm.at[h, 1], erm.at[h, 1], table["E", "m", h] + 1, dev_zd)

    def e_third(h):
        for i in (0, 1):
            eacc[3, i] = e_joined(h, 3, i)
        for i in (0, 1):
            arrived(erp.at[h, i], table["E", "p", h] + i)
            arrived(erm.at[h, i], table["E", "m", h] + i)
        other = 1 - yh
        esy[h] = (eacc[3, other] + erp[h, other].astype(F32) + erm[h, other].astype(F32)).astype(BF16)
        send(esy.at[h], ery.at[h], table["E", "y", h], dev_yp)
        eacc[3, yh] = eacc[3, yh] + erp[h, yh].astype(F32) + erm[h, yh].astype(F32)

    def e_fourth(h):
        arrived(ery.at[h], table["E", "y", h])
        total = eacc[3, yh] + ery[h].astype(F32)
        fgrad_ref[:, h * half:(h + 1) * half] = total.T.astype(BF16)

    wc, wz, wy = width // 2, width // 8, width // 32
    wl = width // 4

    def at(i, n):
        return pl.ds(pl.multiple_of(i * n, n), n)

    def w_core():
        send(wpart.at[at(1 - co, wc)], wrc, table["W", "rc"], dev_sib)

    def w_z():
        arrived(wrc, table["W", "rc"])
        wpart[at(co, wc)] = wpart[at(co, wc)] + wrc[...]
        wzb[...] = wpart[at(co, wc)].astype(BF16)
        for k in (1, 2, 3):
            send(wzb.at[at(turn(z, k), wz)], wrz.at[k - 1], table["W", "rz"] + k - 1, zpeers[k - 1])

    def w_y():
        w2[...] = wpart[pl.ds(pl.multiple_of(co * wc + z * wz, wz), wz)]
        for k in range(3):
            arrived(wrz.at[k], table["W", "rz"] + k)
            w2[...] += wrz[k].astype(F32)
        for k in (1, 2, 3):
            send(w2.at[at(turn(y, k), wy)], wry.at[k - 1], table["W", "ry"] + k - 1, ypeers[k - 1])

    def w_x():
        total = w2[at(y, wy)]
        for k in range(3):
            arrived(wry.at[k], table["W", "ry"] + k)
            total = total + wry[k]
        w3[...] = total
        for k in (1, 2, 3):
            send(w3.at[:, at(turn(x, k), wl)], wrx.at[k - 1], table["W", "rx"] + k - 1, xpeers[k - 1])

    first_z = pl.ds(pl.multiple_of(co * wc + z * wz, wz), wz)

    def row_at(y_):
        return pl.ds(pl.multiple_of(co * wc + z * wz + y_ * wy, wy), wy)

    def w_gx():
        total = w3[:, at(x, wl)]
        for k in range(3):
            arrived(wrx.at[k], table["W", "rx"] + k)
            total = total + wrx[k]
        wfull[row_at(y), at(x, wl)] = total.astype(BF16)
        block = wfull.at[row_at(y), at(x, wl)]
        for k in range(3):
            send(block, block, table["W", "gx"] + k, xpeers[k])

    def w_gy():
        for k in (1, 2, 3):
            arrived(wfull.at[row_at(y), at(turn(x, 4 - k), wl)], table["W", "gx"] + k - 1)
        block = wfull.at[row_at(y)]
        for k in range(3):
            send(block, block, table["W", "gy"] + k, ypeers[k])

    def w_gz():
        for k in (1, 2, 3):
            arrived(wfull.at[row_at(turn(y, 4 - k))], table["W", "gy"] + k - 1)
        block = wfull.at[first_z]
        for k in range(3):
            send(block, block, table["W", "gz"] + k, zpeers[k])

    def w_gc():
        for k in (1, 2, 3):
            where = pl.multiple_of(co * wc + turn(z, 4 - k) * wz, wz)
            arrived(wfull.at[pl.ds(where, wz)], table["W", "gz"] + k - 1)
        block = wfull.at[at(co, wc)]
        send(block, block, table["W", "gc"], dev_sib)

    def w_end():
        arrived(wfull.at[at(1 - co, wc)], table["W", "gc"])
        wgrad_ref[...] = wfull[...].astype(F32) * scale

    a_own(0)
    a_own(1)
    densify(0, 6)
    a_par(0)
    densify(6, 10)
    a_par(1)
    a_ring(0)
    densify(10, NDOM)
    a_ring(1)
    a_far(0)
    a_end(0)
    b_first(0)
    b_part(0, 1, xu)
    b_part(0, 2, xd)
    a_far(1)
    b_part(0, 3, x)
    b_second(0)
    a_end(1)
    b_third(0)
    b_first_1 = lambda: b_first(1)
    b_fourth(0)
    b_first_1()
    b_part(1, 1, xu)
    b_part(1, 2, xd)
    b_second(1)
    b_part(1, 3, x)
    b_third(1)
    b_fourth(1)

    preact[...] = jnp.dot(agg[...], w_ref[...], preferred_element_type=F32)
    pre = preact[...]
    sig = 1.0 / (1.0 + jnp.exp(-pre))
    act_ref[...] = (pre * sig).astype(BF16)
    grad = (cot_ref[...].astype(F32) * (sig * (1.0 + pre * (1.0 - sig)))).astype(BF16)
    for h in (0, 1):
        gbuf[h, :, d_slot("own")] = lax.dot_general(
            w_ref[h * half:(h + 1) * half, :], grad, (((1,), (1,)), ((), ())),
            preferred_element_type=F32).astype(BF16)
        d_own(h)
    wpart[...] = lax.dot_general(
        agg[...], grad, (((0,), (0,)), ((), ())), preferred_element_type=F32)
    w_core()

    d_par(0)
    d_par(1)
    w_z()
    d_ring(0)
    d_ring(1)
    d_far(0)
    e_part(0, 0)
    w_y()
    e_part(0, 1)
    e_first(0)
    d_far(1)
    e_part(0, 2)
    w_x()
    e_part(0, 3)
    e_second(0)
    e_part_1 = lambda kind: e_part(1, kind)
    w_gx()
    e_third(0)
    w_gy()
    e_fourth(0)
    e_part_1(0)
    e_part_1(1)
    e_first(1)
    w_gz()
    e_part_1(2)
    e_part_1(3)
    e_second(1)
    w_gc()
    e_third(1)
    w_end()
    e_fourth(1)
    for copy in pending:
        copy.wait_send()


def local(features, cotangent, weight, tiles, tile_rows, tile_cols, tile_counts):
    rows, width = features.shape
    slots, tile = tiles.shape[3], tiles.shape[-1]
    half = width // 2
    place = tile_rows[0, 0] * 2 + tile_cols[0, 0]
    order = jnp.arange(slots, dtype=jnp.int32)
    target = jnp.concatenate(
        [place, jnp.broadcast_to(jnp.arange(4 * NREP, dtype=jnp.int32), (NDOM, 4 * NREP))], axis=1)
    limit = jnp.concatenate([order, jnp.full((4 * NREP,), slots, jnp.int32)])
    limit = jnp.minimum(limit[None, :], tile_counts[0, 0][:, None])
    match = (place[:, None, :] == target[:, :, None]) & (order[None, None, :] < limit[:, :, None])
    chain = jnp.max(jnp.where(match, order[None, None, :], -1), axis=2)
    chain = jnp.where(chain < 0, slots, chain)

    table, count = message_table()
    dims = (rows, width, tile, slots)
    vmem = pltpu.VMEM
    scratch = [
        vmem((NDOM, slots, tile, tile), BF16),
        vmem((slots + 1, tile, tile), F32),
        vmem((NREP * rows, NDOM * rows), BF16),
        vmem((2, NDOM * rows, half), BF16),
        vmem((2, half, NREP * rows), BF16),
        vmem((4, 2, rows, half), F32),
        vmem((4, 2, half, rows), F32),
        vmem((rows, width), BF16),
        vmem((rows, width), F32),
        vmem((2, 2, rows, half), BF16),
        vmem((2, 2, rows, half), BF16),
        vmem((2, 2, rows, half), BF16),
        vmem((2, rows, half), BF16),
        vmem((2, rows, half), BF16),
        vmem((2, rows, half), BF16),
        vmem((2, 2, rows, half), BF16),
        vmem((2, 2, rows, half), BF16),
        vmem((2, rows, half), BF16),
        vmem((2, 4, 2, half, rows), BF16),
        vmem((2, 2, half, rows), BF16),
        vmem((2, 2, half, rows), BF16),
        vmem((2, 2, half, rows), BF16),
        vmem((2, half, rows), BF16),
        vmem((2, 4, 2, half, rows), BF16),
        vmem((2, half, rows), BF16),
        vmem((2, half, rows), BF16),
        vmem((2, 2, half, rows), BF16),
        vmem((2, 2, half, rows), BF16),
        vmem((2, half, rows), BF16),
        vmem((width, width), F32),
        vmem((width // 2, width), F32),
        vmem((width // 2, width), BF16),
        vmem((3, width // 8, width), BF16),
        vmem((width // 8, width), F32),
        vmem((3, width // 32, width), F32),
        vmem((width // 32, width), F32),
        vmem((3, width // 32, width // 4), F32),
        vmem((width, width), BF16),
        pltpu.SemaphoreType.DMA((NDOM,)),
        pltpu.SemaphoreType.DMA((2,)),
        pltpu.SemaphoreType.DMA((count,)),
        pltpu.SemaphoreType.DMA((count,)),
    ]
    whole = pl.BlockSpec(memory_space=pltpu.VMEM)
    anywhere = pl.BlockSpec(memory_space=pl.ANY)
    return pl.pallas_call(
        functools.partial(kernel, dims, table),
        out_shape=(
            jax.ShapeDtypeStruct((rows, width), BF16),
            jax.ShapeDtypeStruct((rows, width), BF16),
            jax.ShapeDtypeStruct((width, width), F32),
        ),
        in_specs=[pl.BlockSpec(memory_space=pltpu.SMEM), anywhere, whole, whole, anywhere],
        out_specs=(whole, whole, whole),
        scratch_shapes=scratch,
        compiler_params=pltpu.CompilerParams(
            collective_id=0, has_side_effects=True, vmem_limit_bytes=67043328),
    )(chain, features, cotangent, weight, tiles[0, 0])


def solution(mesh):
    in_specs = (
        P(("dom", "repl"), None),
        P(("dom", "repl"), None),
        P(),
        P("dom", "repl", None, None, None, None),
        P("dom", "repl", None, None),
        P("dom", "repl", None, None),
        P("dom", "repl", None),
    )
    out_specs = (P(("dom", "repl"), None), P(("dom", "repl"), None), P())
    return jax.shard_map(local, mesh=mesh, in_specs=in_specs, out_specs=out_specs, check_vma=False)
```

time: 802 us -> 133 us (0.17)
  waiting for transfers between devices: 358 us -> 0 us
  matrix products: 228 us -> 0 us
  local copies, waits for them, and re-layouts: 134 us -> 5.6 us
  Pallas kernels: 0 us -> 124 us
  other arithmetic: 60.5 us -> 2.19 us
  between operations: 13.8 us -> 0.65 us
    dot_general x67 -> x0, matrix products: 228 us -> none  [the longest x32 160 us: place_tiles(): jnp.einsum('rt,taf->raf', selector, prod, precision=lax.Precision.HIGHEST)]
    psum x1 -> x0, waiting for transfers between devices: 144 us -> none  [local(): weight_grad = lax.psum(weight_part, ('dom', 'repl')) * scale]
    ppermute x30 -> x0, waiting for transfers between devices: 125 us -> none  [shifted(): lax.ppermute(x, axis, [(i, (i + by) % length) for i in range(length)])]
    pallas_call x0 -> x1, Pallas kernels: none -> 124 us  [local(): pl.pallas_call(functools.partial(kernel, dims, table), out_shape=(jax.Sha...]
    reduce_scatter x1 -> x0, waiting for transfers between devices: 49.7 us -> none  [local(): own_rows = lax.psum_scatter(totals, 'repl', scatter_dimension=0, tiled=True)]
    gather x32 -> x0, local copies, waits for them, and re-layouts: 47.2 us -> none  [the longest x16 36.4 us: backward_block(): picked = grad_tiles[row_index[column]]]
    while x76 -> x0, local copies, waits for them, and re-layouts: 41.8 us -> none
    all_gather x1 -> x0, waiting for transfers between devices: 40.4 us -> none  [local(): block_grad = lax.all_gather(agg_grad, 'repl', axis=0, tiled=True)]
  transfers between devices with their start and end apart: 33 -> 0, of which waited for: 33 -> 0; matrix products, arithmetic and copies ran while one was open for 26% -> 0% of each run, Pallas kernels for 0% -> 0%
where the time goes in v1:
time: 133 us
  Pallas kernels  124 us (93%)
  local copies, waits for them, and re-layouts  5.6 us (4%)
  other arithmetic  2.19 us (2%)
    pallas_call x1, Pallas kernels, local(): pl.pallas_call(functools.partial(kernel, dims, table), out_shape=(jax.Sha...  124 us
    unnamed x3, local copies, waits for them, and re-layouts  5.6 us

profile of v1, /device:TPU:0, one launch (start us, length us, event | category | flops | bytes accessed | tf_op | source)
XLA Modules:
  0.0 132.8 jit_solution(8245953049135293969)
XLA Ops:
  0.6 0.7 add_bitcast_fusion
  1.4 0.7 pad_add_fusion
  2.1 0.1 select_reduce_fusion
  2.2 0.6 compare_select_fusion.chain_ref
  2.8 124.4 %shard_map.94 = (bf16[256,512]{1,0:T(8,128)(2,1)}, bf16[256,512]{1,0:T(8,128)(2,1)}, f32[512,512]{1,0:T(8,128)}) custom-call(s32[16,48]{1,0:T(8,128)} %compare_select_fusion.chain_ref, bf16[256,512]{1,0:T(8,128)(2,1)} %feat_ref.1, bf16[256,512]{1,0:T(8,128)(2,1)} %cot_ref.1, bf16[512,512]{1,0:T(8,128)(2,1)} %w_ref.1, bf16[16,16,128,128]{3,2,1,0:T(8,128)(2,1)} %bitcast.4), custom_call_target="tpu_custom_call" | custom-call | tf_op jit(solution)/shard_map/pallas_call | solution.py:526
  127.2 1.7 %copy.13 = bf16[256,512]{1,0:T(8,128)(2,1)} copy(bf16[256,512]{1,0:T(8,128)(2,1)} %get-tuple-element.8) | data formatting | bytes 524288
  128.9 1.7 %copy.14 = bf16[256,512]{1,0:T(8,128)(2,1)} copy(bf16[256,512]{1,0:T(8,128)(2,1)} %get-tuple-element.9) | data formatting | bytes 524288
  130.6 2.3 %copy.15 = f32[512,512]{1,0:T(8,128)} copy(f32[512,512]{1,0:T(8,128)} %get-tuple-element.10) | data formatting | bytes 2097152
  (1 shorter events, 0.0 us)

commit v2 on v0

v2 whole, which is shorter than its diff:
```python
import functools

import jax
import jax.numpy as jnp
from jax import lax
from jax.experimental import pallas as pl
from jax.experimental.pallas import tpu as pltpu
from jax.sharding import PartitionSpec as P

F32 = jnp.float32
BF16 = jnp.bfloat16
MESH = pl.DeviceIdType.MESH
Z, YH, CO, YL, X = 4, 2, 2, 2, 4
NDOM, NREP = Z * YH * CO, YL * X
VMEM_LIMIT = 60 << 20


class Names:
    def __init__(self):
        self.count = 0

    def take(self, n=1):
        base = self.count
        self.count += n
        return base


def message_table():
    names = Names()
    table = {}
    gather = ("y0", "y1", "nu0", "nu1", "nd0", "nd1", "fu", "fd", "hd", "hu", "pu", "pd", "qu", "qd")
    reduce = ("f0u", "f0d", "f1u", "f1d", "yu", "yd", "tu", "td", "ou0", "ou1", "od0", "od1", "y0", "y1")
    for h in (0, 1):
        for phase, kinds, siblings in (("A", gather, 8), ("B", reduce, 0), ("D", gather, 0), ("E", reduce, 8)):
            for kind in kinds:
                table[phase, kind, h] = names.take()
            if siblings:
                table[phase, "sib", h] = names.take(siblings)
    for kind in ("rc", "gc"):
        table["W", kind] = names.take(1)
    for kind in ("rz", "ry", "rx", "gx", "gy", "gz"):
        table["W", kind] = names.take(3)
    return table, names.count


def kernel(dims, table, trow_ref, tcol_ref, count_ref, feat_ref, cot_ref, w_ref, tiles_ref,
           act_ref, grad_ref, wgrad_ref, *scratch):
    rows, width, tile, slots = dims
    half = width // 2
    (tbuf, rbuf, adj, fbuf, gbuf, pacc, eacc, agg, preact,
     bs_far, bs_y0, bs_t, bs_o, bs_y, br_far, br_y0, br_t, br_o, br_y,
     es_far, es_y0, es_t, es_o, es_y, er_far, er_y0, er_t, er_o, er_y, ess, ers,
     wpart, wrc, wzb, wrz, w2, wry, w3, wrx, wfull,
     wanted, links, chain_ref,
     tsem, fsem, csem, ssem, rsem) = scratch

    dom = lax.axis_index("dom")
    rep = lax.axis_index("repl")
    co = lax.rem(dom, 2)
    yh = lax.rem(lax.div(dom, 2), 2)
    z = lax.div(dom, 4)
    x = lax.rem(rep, 4)
    yl = lax.div(rep, 4)
    y = yh * 2 + yl

    def turn(v, by):
        return lax.rem(v + by, 4)

    zu, zd, z2 = turn(z, 1), turn(z, 3), turn(z, 2)
    xu, xd, x2 = turn(x, 1), turn(x, 3), turn(x, 2)

    def did(z_, yh_, co_):
        return z_ * 4 + yh_ * 2 + co_

    def at_y(y_):
        return (did(z, lax.div(y_, 2), co), lax.rem(y_, 2) * 4 + x)

    dev_sib = (did(z, yh, 1 - co), rep)
    dev_zu, dev_zd = (did(zu, yh, co), rep), (did(zd, yh, co), rep)
    dev_yp = (did(z, 1 - yh, co), rep)
    dev_xu, dev_xd = (dom, yl * 4 + xu), (dom, yl * 4 + xd)
    dev_yl = (dom, (1 - yl) * 4 + x)
    zpeers = [(did(turn(z, k), yh, co), rep) for k in (1, 2, 3)]
    ypeers = [at_y(turn(y, k)) for k in (1, 2, 3)]
    xpeers = [(dom, yl * 4 + turn(x, k)) for k in (1, 2, 3)]

    pending = []

    def send(src, dst, number, dev, slot=None):
        arrival = number if slot is None else number + slot
        copy = pltpu.make_async_remote_copy(
            src_ref=src, dst_ref=dst, send_sem=ssem.at[len(pending)], recv_sem=rsem.at[arrival],
            device_id=dev, device_id_type=MESH)
        copy.start()
        pending.append(copy)

    def arrived(dst, number, slot=None):
        number = number if slot is None else number + slot
        pltpu.make_async_remote_copy(
            src_ref=dst, dst_ref=dst, send_sem=ssem.at[0], recv_sem=rsem.at[number],
            device_id=dev_sib, device_id_type=MESH).wait_recv()

    def slab(c):
        return pl.ds(pl.multiple_of(c * rows, rows), rows)

    for h in (0, 1):
        pltpu.make_async_copy(
            feat_ref.at[:, h * half:(h + 1) * half], fbuf.at[h, slab(dom)], fsem.at[h]).start()
    for c in range(NDOM):
        pltpu.make_async_copy(tiles_ref.at[c], tbuf.at[c], tsem.at[c]).start()
    barrier = pltpu.get_barrier_semaphore()
    partners = [dev_sib] + zpeers + ypeers + xpeers
    for dev in partners:
        pl.semaphore_signal(barrier, inc=1, device_id=dev, device_id_type=MESH)
    rbuf[slots] = jnp.zeros((tile, tile), F32)

    place = trow_ref[...] * 2 + tcol_ref[...]
    lane = lax.broadcasted_iota(jnp.int32, (NDOM, 128), 1)
    wanted[...] = lane - slots
    wanted[:, :slots] = place
    target = wanted[...]
    square = (NDOM, NDOM)
    diagonal = lax.broadcasted_iota(jnp.int32, square, 0) == lax.broadcasted_iota(jnp.int32, square, 1)
    live = jnp.sum(jnp.where(diagonal, count_ref[...], 0), axis=1, keepdims=True)
    limit = jnp.minimum(jnp.where(lane < slots, lane, slots), live)
    chain = jnp.full((NDOM, 128), slots, jnp.int32)
    for t in range(slots):
        chain = jnp.where((target == place[:, t:t + 1]) & (t < limit), t, chain)
    links[...] = chain
    pl.semaphore_wait(barrier, len(partners))
    load = pltpu.make_async_copy(links, chain_ref, csem)
    load.start()

    def part_of(n, part):
        return pl.ds(0, n) if part is None else pl.ds(part * (n // 2), n // 2)

    def gather(phase, view, dev_u, dev_d, dev_y, after):
        def push(h, kind, dev, *where):
            block = view(h, *where)
            send(block, block, table[phase, kind, h], dev)

        def wait(h, kind, *where):
            arrived(view(h, *where), table[phase, kind, h])

        def pair(h):
            for part in (0, 1):
                push(h, f"y{part}", dev_y, "me", 1, part)
            after(h, "me", 1)

        def near(h, turn_):
            push(h, f"nu{turn_}", dev_u, "me", 1, turn_)
            push(h, f"nd{1 - turn_}", dev_d, "me", 1, 1 - turn_)

        def far(h):
            wait(h, "nu0", "d", 1, 0)
            push(h, "fu", dev_u, "d", 1, 0)
            wait(h, "nd1", "u", 1, 1)
            push(h, "fd", dev_d, "u", 1, 1)

        def side(h):
            wait(h, "nu1", "d", 1, 1)
            push(h, "hd", dev_y, "d", 1, 1)
            wait(h, "nd0", "u", 1, 0)
            push(h, "hu", dev_y, "u", 1, 0)
            after(h, "d", 1)
            after(h, "u", 1)

        def other(h):
            wait(h, "y0", "me", 0, 0)
            push(h, "pu", dev_u, "me", 0, 0)
            wait(h, "y1", "me", 0, 1)
            push(h, "pd", dev_d, "me", 0, 1)
            after(h, "me", 0)

        def far_other(h):
            wait(h, "pu", "d", 0, 0)
            push(h, "qu", dev_u, "d", 0, 0)
            wait(h, "pd", "u", 0, 1)
            push(h, "qd", dev_d, "u", 0, 1)

        def rest(h):
            wait(h, "hd", "d", 0, 1)
            wait(h, "hu", "u", 0, 0)
            after(h, "d", 0)
            after(h, "u", 0)
            wait(h, "fu", "2", 1, 0)
            wait(h, "fd", "2", 1, 1)
            after(h, "2", 1)
            wait(h, "qu", "2", 0, 0)
            wait(h, "qd", "2", 0, 1)
            after(h, "2", 0)

        return pair, near, far, side, other, far_other, rest

    FAR, UP, DOWN, HERE = 0, 1, 2, 3

    def reduce(phase, n, value, acc, buffers, dev_u, dev_d, dev_y):
        s_far, s_y0, s_t, s_o, s_y, r_far, r_y0, r_t, r_o, r_y = buffers
        a, b = part_of(n, 0), part_of(n, 1)

        def push(src, dst, h, kind, dev):
            send(src, dst, table[phase, kind, h], dev)

        def far(h):
            for q in (0, 1):
                s_far[h, q] = value(h, FAR, q, part_of(n, None)).astype(BF16)
                push(s_far.at[h, q, a], r_far.at[h, q, 0], h, f"f{q}u", dev_u)
                push(s_far.at[h, q, b], r_far.at[h, q, 1], h, f"f{q}d", dev_d)

        def pair_up(h):
            s_y0[h, 0] = value(h, UP, 0, b).astype(BF16)
            push(s_y0.at[h, 0], r_y0.at[h, 0], h, "yu", dev_y)

        def pair_down(h):
            s_y0[h, 1] = value(h, DOWN, 0, a).astype(BF16)
            push(s_y0.at[h, 1], r_y0.at[h, 1], h, "yd", dev_y)

        def other(h):
            above, below = value(h, UP, 0, a), value(h, DOWN, 0, b)
            arrived(r_far.at[h, 0, 0], table[phase, "f0u", h])
            s_t[h, 0] = (above + r_far[h, 0, 0].astype(F32)).astype(BF16)
            push(s_t.at[h, 0], r_t.at[h, 0], h, "tu", dev_u)
            arrived(r_far.at[h, 0, 1], table[phase, "f0d", h])
            s_t[h, 1] = (below + r_far[h, 0, 1].astype(F32)).astype(BF16)
            push(s_t.at[h, 1], r_t.at[h, 1], h, "td", dev_d)

        def own(h):
            for i, (kind, dev, name, one, two) in enumerate(((UP, dev_u, "u", a, b), (DOWN, dev_d, "d", b, a))):
                value_one, value_two = value(h, kind, 1, one), value(h, kind, 1, two)
                arrived(r_far.at[h, 1, i], table[phase, f"f1{name}", h])
                s_o[h, i, one] = (value_one + r_far[h, 1, i].astype(F32)).astype(BF16)
                push(s_o.at[h, i, one], r_o.at[h, i, one], h, f"o{name}0", dev)
                arrived(r_y0.at[h, i], table[phase, f"y{name}", h])
                s_o[h, i, two] = (value_two + r_y0[h, i].astype(F32)).astype(BF16)
                push(s_o.at[h, i, two], r_o.at[h, i, two], h, f"o{name}1", dev)

        def pair(h):
            for i, (name, rows_) in enumerate((("u", a), ("d", b))):
                arrived(r_t.at[h, i], table[phase, f"t{name}", h])
                s_y[h, rows_] = (value(h, HERE, 0, rows_) + r_t[h, i].astype(F32)).astype(BF16)
                push(s_y.at[h, rows_], r_y.at[h, rows_], h, f"y{i}", dev_y)

        def collect(h):
            total = value(h, HERE, 1, part_of(n, None))
            for i, (name, one, two) in enumerate((("u", a, b), ("d", b, a))):
                arrived(r_o.at[h, i, one], table[phase, f"o{name}0", h])
                arrived(r_o.at[h, i, two], table[phase, f"o{name}1", h])
            acc[h, HERE, 1] = total + r_o[h, 0].astype(F32) + r_o[h, 1].astype(F32)

        def end(h):
            arrived(r_y.at[h, a], table[phase, "y0", h])
            arrived(r_y.at[h, b], table[phase, "y1", h])
            return acc[h, HERE, 1] + r_y[h].astype(F32)

        return far, pair_up, pair_down, other, own, pair, collect, end

    a_places = [("me", 1), ("me", 0), ("d", 1), ("u", 1), ("d", 0), ("u", 0), ("2", 1), ("2", 0)]

    def a_slot(place, column, core):
        return did({"me": z, "u": zu, "d": zd, "2": z2}[place], yh if column else 1 - yh, core)

    def a_view(h, place, column, part):
        start = a_slot(place, column, co) * rows + (0 if part is None else part * (rows // 2))
        size = rows if part is None else rows // 2
        return fbuf.at[h, pl.ds(pl.multiple_of(start, size), size)]

    def a_after(h, place, column):
        block = a_view(h, place, column, None)
        send(block, block, table["A", "sib", h] + a_places.index((place, column)), dev_sib)

    a_pair, a_near, a_far, a_side, a_other, a_far_other, a_rest = gather("A", a_view, dev_zu, dev_zd, dev_yp, a_after)

    def a_open(h):
        pltpu.make_async_copy(
            feat_ref.at[:, h * half:(h + 1) * half], fbuf.at[h, slab(dom)], fsem.at[h]).wait()
        a_pair(h)

    def a_end(h):
        for i, (place, column) in enumerate(a_places):
            arrived(fbuf.at[h, slab(a_slot(place, column, 1 - co))], table["A", "sib", h] + i)

    def densify(first, last):
        @pl.loop(first, last)
        def _(c):
            pltpu.make_async_copy(tiles_ref.at[c], tbuf.at[c], tsem.at[c]).wait()
            for t in range(slots):
                rbuf[t] = tbuf[c, t].astype(F32) + rbuf[chain_ref[c, t]]
            for p in range(4 * NREP):
                r, k = p // 2, p % 2
                g, i = r // 2, r % 2
                row = ((g % 4 * 2 + g // 4) * 2 + i) * tile
                lane = pl.multiple_of(c * rows + k * tile, tile)
                adj[row:row + tile, pl.ds(lane, tile)] = rbuf[chain_ref[c, slots + p]].astype(BF16)

    def b_part(h, kind):
        x_ = (x2, xu, xd, x)[kind]

        @pl.loop(0, 2)
        def _(i):
            parity = i * yl + (1 - i) * (1 - yl)
            where = pl.multiple_of((x_ * 2 + parity) * rows, rows)
            pacc[h, kind, i] = jnp.dot(adj[pl.ds(where, rows), :], fbuf[h], preferred_element_type=F32)

    def b_value(h, kind, q, part):
        return pacc[h, kind, q, part]

    b_far, b_pair_up, b_pair_down, b_other, b_own, b_pair, b_collect, b_end = reduce(
        "B", rows, b_value, pacc, (bs_far, bs_y0, bs_t, bs_o, bs_y, br_far, br_y0, br_t, br_o, br_y),
        dev_xu, dev_xd, dev_yl)

    def b_close(h):
        agg[:, h * half:(h + 1) * half] = b_end(h).astype(BF16)

    def d_view(h, place, column, part):
        slot = {"me": x, "u": xu, "d": xd, "2": x2}[place] * 2 + (yl if column else 1 - yl)
        return gbuf.at[h, part_of(half, part), pl.ds(pl.multiple_of(slot * rows, rows), rows)]

    d_pair, d_near, d_far, d_side, d_other, d_far_other, d_rest = gather(
        "D", d_view, dev_xu, dev_xd, dev_yl, lambda h, place, column: None)

    def e_part(h, kind):
        z_ = (z2, zu, zd, z)[kind]

        @pl.loop(0, 2)
        def _(i):
            parity = i * yh + (1 - i) * (1 - yh)
            ess[h, kind, i] = jnp.dot(
                gbuf[h], adj[:, slab(did(z_, parity, 1 - co))], preferred_element_type=F32).astype(BF16)
            eacc[h, kind, i] = jnp.dot(
                gbuf[h], adj[:, slab(did(z_, parity, co))], preferred_element_type=F32)

        for i in (0, 1):
            send(ess.at[h, kind, i], ers.at[h, kind, i], table["E", "sib", h] + kind * 2 + i, dev_sib)

    def e_join(h, kind):
        for i in (0, 1):
            arrived(ers.at[h, kind, i], table["E", "sib", h] + kind * 2 + i)

    def e_value(h, kind, q, part):
        return eacc[h, kind, q, part] + ers[h, kind, q, part].astype(F32)

    e_far, e_pair_up, e_pair_down, e_other, e_own, e_pair, e_collect, e_end = reduce(
        "E", half, e_value, eacc, (es_far, es_y0, es_t, es_o, es_y, er_far, er_y0, er_t, er_o, er_y),
        dev_zu, dev_zd, dev_yp)

    def e_close(h):
        grad_ref[h * half:(h + 1) * half, :] = e_end(h).astype(BF16)

    wc, wz, wy = width // 2, width // 8, width // 32
    wl = width // 4

    def at(i, n):
        return pl.ds(pl.multiple_of(i * n, n), n)

    def w_core():
        send(wpart.at[at(1 - co, wc)], wrc, table["W", "rc"], dev_sib)

    def first_at(y_):
        return pl.ds(pl.multiple_of(co * wc + y_ * wz, wz), wz)

    def row_at(z_):
        return pl.ds(pl.multiple_of(co * wc + y * wz + z_ * wy, wy), wy)

    def w_y():
        arrived(wrc, table["W", "rc"])
        wpart[at(co, wc)] = wpart[at(co, wc)] + wrc[...]
        wzb[...] = wpart[at(co, wc)].astype(BF16)
        for k in (1, 2, 3):
            send(wzb.at[at(turn(y, k), wz)], wrz.at[k - 1], table["W", "ry"] + k - 1, ypeers[k - 1])

    def w_z():
        w2[...] = wpart[first_at(y)]
        for k in range(3):
            arrived(wrz.at[k], table["W", "ry"] + k)
            w2[...] += wrz[k].astype(F32)
        for k in (1, 2, 3):
            send(w2.at[at(turn(z, k), wy)], wry.at[k - 1], table["W", "rz"] + k - 1, zpeers[k - 1])

    def w_x():
        total = w2[at(z, wy)]
        for k in range(3):
            arrived(wry.at[k], table["W", "rz"] + k)
            total = total + wry[k]
        w3[...] = total
        for k in (1, 2, 3):
            send(w3.at[:, at(turn(x, k), wl)], wrx.at[k - 1], table["W", "rx"] + k - 1, xpeers[k - 1])

    def w_gx():
        total = w3[:, at(x, wl)]
        for k in range(3):
            arrived(wrx.at[k], table["W", "rx"] + k)
            total = total + wrx[k]
        wfull[row_at(z), at(x, wl)] = total.astype(BF16)
        block = wfull.at[row_at(z), at(x, wl)]
        for k in range(3):
            send(block, block, table["W", "gx"] + k, xpeers[k])

    def w_gz():
        for k in (1, 2, 3):
            arrived(wfull.at[row_at(z), at(turn(x, 4 - k), wl)], table["W", "gx"] + k - 1)
        block = wfull.at[row_at(z)]
        for k in range(3):
            send(block, block, table["W", "gz"] + k, zpeers[k])

    def w_gy():
        for k in (1, 2, 3):
            arrived(wfull.at[row_at(turn(z, 4 - k))], table["W", "gz"] + k - 1)
        block = wfull.at[first_at(y)]
        for k in range(3):
            send(block, block, table["W", "gy"] + k, ypeers[k])

    def w_gc():
        for k in (1, 2, 3):
            arrived(wfull.at[first_at(turn(y, 4 - k))], table["W", "gy"] + k - 1)
        block = wfull.at[at(co, wc)]
        send(block, block, table["W", "gc"], dev_sib)

    def w_end():
        arrived(wfull.at[at(1 - co, wc)], table["W", "gc"])
        wgrad_ref[...] = wfull[...]

    a_open(0)
    a_near(0, 0)
    a_near(0, 1)
    a_open(1)
    a_near(1, 0)
    load.wait()
    densify(0, 6)
    a_far(0)
    a_other(0)
    a_near(1, 1)
    a_side(0)
    densify(6, 10)
    a_other(1)
    a_far_other(0)
    a_far(1)
    a_side(1)
    densify(10, NDOM)
    a_far_other(1)
    a_rest(0)
    a_end(0)
    b_part(0, FAR)
    b_far(0)
    b_part(0, UP)
    b_pair_up(0)
    a_rest(1)
    b_part(0, DOWN)
    b_pair_down(0)
    a_end(1)
    b_other(0)
    b_part(1, FAR)
    b_far(1)
    b_own(0)
    b_part(1, UP)
    b_pair_up(1)
    b_part(1, DOWN)
    b_pair_down(1)
    b_part(0, HERE)
    b_pair(0)
    b_other(1)
    b_part(1, HERE)
    b_own(1)
    b_collect(0)
    b_pair(1)
    b_close(0)
    preact[...] = jnp.dot(agg[:, :half], w_ref[:half, :], preferred_element_type=F32)
    b_collect(1)
    b_close(1)

    pre = preact[...] + jnp.dot(agg[:, half:], w_ref[half:, :], preferred_element_type=F32)
    sig = 1.0 / (1.0 + jnp.exp(-pre))
    act_ref[...] = (pre * sig).astype(BF16)
    grad = (cot_ref[...].astype(F32) * (sig * (1.0 + pre * (1.0 - sig)))).astype(BF16)
    for h in (0, 1):
        gbuf[h, :, pl.ds(pl.multiple_of((x * 2 + yl) * rows, rows), rows)] = lax.dot_general(
            w_ref[h * half:(h + 1) * half, :], grad, (((1,), (1,)), ((), ())),
            preferred_element_type=F32).astype(BF16)
        d_pair(h)
        d_near(h, 0)
        if h == 0:
            d_near(h, 1)
    wpart[...] = lax.dot_general(
        agg[...], grad, (((0,), (0,)), ((), ())), preferred_element_type=F32)
    w_core()

    d_far(0)
    d_other(0)
    d_near(1, 1)
    d_side(0)
    w_y()
    d_other(1)
    d_far_other(0)
    d_far(1)
    d_side(1)
    w_z()
    d_far_other(1)
    d_rest(0)
    e_part(0, FAR)
    e_part(0, UP)
    e_join(0, FAR)
    e_far(0)
    w_x()
    e_part(0, DOWN)
    e_join(0, UP)
    e_pair_up(0)
    d_rest(1)
    e_part(1, FAR)
    e_join(0, DOWN)
    e_pair_down(0)
    e_other(0)
    e_part(1, UP)
    e_join(1, FAR)
    e_far(1)
    w_gx()
    e_own(0)
    e_part(1, DOWN)
    e_join(1, UP)
    e_pair_up(1)
    w_gz()
    e_part(0, HERE)
    e_join(1, DOWN)
    e_pair_down(1)
    e_other(1)
    e_join(0, HERE)
    e_pair(0)
    e_part(1, HERE)
    w_gy()
    e_own(1)
    e_join(1, HERE)
    e_pair(1)
    e_collect(0)
    w_gc()
    e_close(0)
    e_collect(1)
    w_end()
    e_close(1)
    for copy in pending:
        copy.wait_send()


def reduce_scratch(n, m):
    shapes = [
        [(2, 2, n, m), (2, 2, n // 2, m), (2, 2, n // 2, m), (2, 2, n, m), (2, n, m)],
        [(2, 2, 2, n // 2, m), (2, 2, n // 2, m), (2, 2, n // 2, m), (2, 2, n, m), (2, n, m)],
    ]
    return [pltpu.VMEM(shape, BF16) for side in shapes for shape in side]


def finish(scale, act_ref, grad_t_ref, weight_ref, act_out, fgrad_out, wgrad_out):
    act_out[...] = act_ref[...]
    fgrad_out[...] = grad_t_ref[...].T
    wgrad_out[...] = weight_ref[...].astype(F32) * scale


def local(features, cotangent, weight, tiles, tile_rows, tile_cols, tile_counts):
    rows, width = features.shape
    slots, tile = tiles.shape[3], tiles.shape[-1]
    half = width // 2
    table, count = message_table()
    dims = (rows, width, tile, slots)
    vmem = pltpu.VMEM
    scratch = [
        vmem((NDOM, slots, tile, tile), BF16),
        vmem((slots + 1, tile, tile), F32),
        vmem((NREP * rows, NDOM * rows), BF16),
        vmem((2, NDOM * rows, half), BF16),
        vmem((2, half, NREP * rows), BF16),
        vmem((2, 4, 2, rows, half), F32),
        vmem((2, 4, 2, half, rows), F32),
        vmem((rows, width), BF16),
        vmem((rows, width), F32),
        *reduce_scratch(rows, half),
        *reduce_scratch(half, rows),
        vmem((2, 4, 2, half, rows), BF16),
        vmem((2, 4, 2, half, rows), BF16),
        vmem((width, width), F32),
        vmem((width // 2, width), F32),
        vmem((width // 2, width), BF16),
        vmem((3, width // 8, width), BF16),
        vmem((width // 8, width), F32),
        vmem((3, width // 32, width), F32),
        vmem((width // 32, width), F32),
        vmem((3, width // 32, width // 4), F32),
        vmem((width, width), BF16),
        vmem((NDOM, 128), jnp.int32),
        vmem((NDOM, 128), jnp.int32),
        pltpu.SMEM((NDOM, 128), jnp.int32),
        pltpu.SemaphoreType.DMA((NDOM,)),
        pltpu.SemaphoreType.DMA((2,)),
        pltpu.SemaphoreType.DMA,
        pltpu.SemaphoreType.DMA((count,)),
        pltpu.SemaphoreType.DMA((count,)),
    ]
    whole = pl.BlockSpec(memory_space=pltpu.VMEM)
    anywhere = pl.BlockSpec(memory_space=pl.ANY)
    act, grad_t, weight_sum = pl.pallas_call(
        functools.partial(kernel, dims, table),
        out_shape=(
            jax.ShapeDtypeStruct((rows, width), BF16),
            jax.ShapeDtypeStruct((width, rows), BF16),
            jax.ShapeDtypeStruct((width, width), BF16),
        ),
        in_specs=[whole, whole, whole, anywhere, whole, whole, anywhere],
        out_specs=(whole, whole, whole),
        scratch_shapes=scratch,
        compiler_params=pltpu.CompilerParams(
            collective_id=0, has_side_effects=True, vmem_limit_bytes=VMEM_LIMIT),
    )(tile_rows[0, 0], tile_cols[0, 0], tile_counts[0], features, cotangent, weight, tiles[0, 0])
    return pl.pallas_call(
        functools.partial(finish, float(rows * NDOM * NREP) ** (-0.5)),
        out_shape=(
            jax.ShapeDtypeStruct((rows, width), BF16),
            jax.ShapeDtypeStruct((rows, width), BF16),
            jax.ShapeDtypeStruct((width, width), F32),
        ),
        in_specs=[whole, whole, whole],
        out_specs=(whole, whole, whole),
    )(act, grad_t, weight_sum)


def solution(mesh):
    in_specs = (
        P(("dom", "repl"), None),
        P(("dom", "repl"), None),
        P(),
        P("dom", "repl", None, None, None, None),
        P("dom", "repl", None, None),
        P("dom", "repl", None, None),
        P("dom", "repl", None),
    )
    out_specs = (P(("dom", "repl"), None), P(("dom", "repl"), None), P())
    return jax.shard_map(local, mesh=mesh, in_specs=in_specs, out_specs=out_specs, check_vma=False)
```

time: 802 us -> 94.5 us (0.12)
  waiting for transfers between devices: 358 us -> 0 us
  matrix products: 228 us -> 0 us
  local copies, waits for them, and re-layouts: 134 us -> 0 us
  Pallas kernels: 0 us -> 93.3 us
  other arithmetic: 60.5 us -> 0 us
  between operations: 13.8 us -> 0.64 us
    dot_general x67 -> x0, matrix products: 228 us -> none  [the longest x32 160 us: place_tiles(): jnp.einsum('rt,taf->raf', selector, prod, precision=lax.Precision.HIGHEST)]
    psum x1 -> x0, waiting for transfers between devices: 144 us -> none  [local(): weight_grad = lax.psum(weight_part, ('dom', 'repl')) * scale]
    ppermute x30 -> x0, waiting for transfers between devices: 125 us -> none  [shifted(): lax.ppermute(x, axis, [(i, (i + by) % length) for i in range(length)])]
    pallas_call x0 -> x2, Pallas kernels: none -> 93.3 us  [the longest x1 90.9 us: local(): pl.pallas_call(functools.partial(kernel, dims, table), out_shape=(jax.Sha...]
    reduce_scatter x1 -> x0, waiting for transfers between devices: 49.7 us -> none  [local(): own_rows = lax.psum_scatter(totals, 'repl', scatter_dimension=0, tiled=True)]
    gather x32 -> x0, local copies, waits for them, and re-layouts: 47.2 us -> none  [the longest x16 36.4 us: backward_block(): picked = grad_tiles[row_index[column]]]
    while x76 -> x0, local copies, waits for them, and re-layouts: 41.8 us -> none
    all_gather x1 -> x0, waiting for transfers between devices: 40.4 us -> none  [local(): block_grad = lax.all_gather(agg_grad, 'repl', axis=0, tiled=True)]
  transfers between devices with their start and end apart: 33 -> 0, of which waited for: 33 -> 0; matrix products, arithmetic and copies ran while one was open for 26% -> 0% of each run, Pallas kernels for 0% -> 0%
where the time goes in v2:
time: 94.5 us; the launch traced here: 94 us
  Pallas kernels  93.3 us (99%)
    pallas_call x1, Pallas kernels, local(): pl.pallas_call(functools.partial(kernel, dims, table), out_shape=(jax.Sha...  90.9 us
    pallas_call x1, Pallas kernels, local(): pl.pallas_call(functools.partial(finish, float(rows * NDOM * NREP) ** (-0...  2.41 us

profile of v2, /device:TPU:0, one launch (start us, length us, event | category | flops | bytes accessed | tf_op | source)
XLA Modules:
  0.0 94.0 jit_solution(383481872956260520)
XLA Ops:
  0.6 90.9 %shard_map.94 = (bf16[256,512]{1,0:T(8,128)(2,1)}, bf16[512,256]{1,0:T(8,128)(2,1)}, bf16[512,512]{1,0:T(8,128)(2,1)}) custom-call(s32[16,16]{1,0:T(8,128)} %bitcast.5, s32[16,16]{1,0:T(8,128)} %bitcast.6, s32[1,16]{1,0:T(1,128)} %bitcast.7, bf16[256,512]{1,0:T(8,128)(2,1)} %feat_ref.1, bf16[256,512]{1,0:T(8,128)(2,1)} %cot_ref.1, bf16[512,512]{1,0:T(8,128)(2,1)} %w_ref.1, ...), custom_call_target="tpu_custom_call" | custom-call | tf_op jit(solution)/shard_map/pallas_call | solution.py:596
  91.6 2.4 %shard_map.95 = (bf16[256,512]{1,0:T(8,128)(2,1)}, bf16[256,512]{1,0:T(8,128)(2,1)}, f32[512,512]{1,0:T(8,128)}) custom-call(bf16[256,512]{1,0:T(8,128)(2,1)} %get-tuple-element.6.act_ref, bf16[512,256]{1,0:T(8,128)(2,1)} %get-tuple-element.7.grad_t_ref, bf16[512,512]{1,0:T(8,128)(2,1)} %get-tuple-element.8.weight_ref), custom_call_target="tpu_custom_call" | custom-call | tf_op jit(solution)/shard_map/pallas_call | solution.py:609

commit v3 on v2

--- a/solution.py
+++ b/solution.py
@@ -43,7 +43,7 @@
     return table, names.count
 
 
-def kernel(dims, table, trow_ref, tcol_ref, count_ref, feat_ref, cot_ref, w_ref, tiles_ref,
+def kernel(dims, table, trow_ref, tcol_ref, count_ref, feat_ref, cot_any, w_any, tiles_ref,
            act_ref, grad_ref, wgrad_ref, *scratch):
     rows, width, tile, slots = dims
     half = width // 2
@@ -51,7 +51,7 @@
      bs_far, bs_y0, bs_t, bs_o, bs_y, br_far, br_y0, br_t, br_o, br_y,
      es_far, es_y0, es_t, es_o, es_y, er_far, er_y0, er_t, er_o, er_y, ess, ers,
      wpart, wrc, wzb, wrz, w2, wry, w3, wrx, wfull,
-     wanted, links, chain_ref,
+     wanted, links, chain_ref, cot_ref, w_ref, isem,
      tsem, fsem, csem, ssem, rsem) = scratch
 
     dom = lax.axis_index("dom")
@@ -112,6 +112,9 @@
     partners = [dev_sib] + zpeers + ypeers + xpeers
     for dev in partners:
         pl.semaphore_signal(barrier, inc=1, device_id=dev, device_id_type=MESH)
+    loads = [pltpu.make_async_copy(w_any, w_ref, isem.at[0]), pltpu.make_async_copy(cot_any, cot_ref, isem.at[1])]
+    for copy in loads:
+        copy.start()
     rbuf[slots] = jnp.zeros((tile, tile), F32)
 
     place = trow_ref[...] * 2 + tcol_ref[...]
@@ -463,6 +466,8 @@
     b_collect(0)
     b_pair(1)
     b_close(0)
+    for copy in loads:
+        copy.wait()
     preact[...] = jnp.dot(agg[:, :half], w_ref[:half, :], preferred_element_type=F32)
     b_collect(1)
     b_close(1)
@@ -546,10 +551,26 @@
     return [pltpu.VMEM(shape, BF16) for side in shapes for shape in side]
 
 
-def finish(scale, act_ref, grad_t_ref, weight_ref, act_out, fgrad_out, wgrad_out):
-    act_out[...] = act_ref[...]
-    fgrad_out[...] = grad_t_ref[...].T
-    wgrad_out[...] = weight_ref[...].astype(F32) * scale
+def finish(scale, act_in, grad_in, weight_in, act_out, grad_out, weight_out,
+           act, grad, grad_t, weight, weight_f, sem_in, sem_out):
+    moves_in = [
+        pltpu.make_async_copy(src, dst, sem_in.at[i])
+        for i, (src, dst) in enumerate(((weight_in, weight), (grad_in, grad), (act_in, act)))]
+    moves_out = [
+        pltpu.make_async_copy(src, dst, sem_out.at[i])
+        for i, (src, dst) in enumerate(((weight_f, weight_out), (grad_t, grad_out), (act, act_out)))]
+    for move in moves_in:
+        move.start()
+    moves_in[0].wait()
+    weight_f[...] = weight[...].astype(F32) * scale
+    moves_out[0].start()
+    moves_in[1].wait()
+    grad_t[...] = grad[...].T
+    moves_out[1].start()
+    moves_in[2].wait()
+    moves_out[2].start()
+    for move in moves_out:
+        move.wait()
 
 
 def local(features, cotangent, weight, tiles, tile_rows, tile_cols, tile_counts):
@@ -585,6 +606,9 @@
         vmem((NDOM, 128), jnp.int32),
         vmem((NDOM, 128), jnp.int32),
         pltpu.SMEM((NDOM, 128), jnp.int32),
+        vmem((rows, width), BF16),
+        vmem((width, width), BF16),
+        pltpu.SemaphoreType.DMA((2,)),
         pltpu.SemaphoreType.DMA((NDOM,)),
         pltpu.SemaphoreType.DMA((2,)),
         pltpu.SemaphoreType.DMA,
@@ -600,7 +624,7 @@
             jax.ShapeDtypeStruct((width, rows), BF16),
             jax.ShapeDtypeStruct((width, width), BF16),
         ),
-        in_specs=[whole, whole, whole, anywhere, whole, whole, anywhere],
+        in_specs=[whole, whole, whole, anywhere, anywhere, anywhere, anywhere],
         out_specs=(whole, whole, whole),
         scratch_shapes=scratch,
         compiler_params=pltpu.CompilerParams(
@@ -613,8 +637,17 @@
             jax.ShapeDtypeStruct((rows, width), BF16),
             jax.ShapeDtypeStruct((width, width), F32),
         ),
-        in_specs=[whole, whole, whole],
-        out_specs=(whole, whole, whole),
+        in_specs=[anywhere, anywhere, anywhere],
+        out_specs=(anywhere, anywhere, anywhere),
+        scratch_shapes=[
+            vmem((rows, width), BF16),
+            vmem((width, rows), BF16),
+            vmem((rows, width), BF16),
+            vmem((width, width), BF16),
+            vmem((width, width), F32),
+            pltpu.SemaphoreType.DMA((3,)),
+            pltpu.SemaphoreType.DMA((3,)),
+        ],
     )(act, grad_t, weight_sum)
 
 

time: 94.5 us -> 94 us (level)
  no operation moved by 1% of the time
where the time goes in v3:
time: 94 us; the launch traced here: 93.5 us
  Pallas kernels  92.8 us (99%)
    pallas_call x1, Pallas kernels, local(): pl.pallas_call(functools.partial(kernel, dims, table), out_shape=(jax.Sha...  90.5 us
    pallas_call x1, Pallas kernels, local(): pl.pallas_call(functools.partial(finish, float(rows * NDOM * NREP) ** (-0...  2.31 us

profile of v3, /device:TPU:0, one launch (start us, length us, event | category | flops | bytes accessed | tf_op | source)
XLA Modules:
  0.0 93.5 jit_solution(1943638682729089148)
XLA Ops:
  0.6 90.5 %shard_map.94 = (bf16[256,512]{1,0:T(8,128)(2,1)}, bf16[512,256]{1,0:T(8,128)(2,1)}, bf16[512,512]{1,0:T(8,128)(2,1)}) custom-call(s32[16,16]{1,0:T(8,128)} %bitcast.5, s32[16,16]{1,0:T(8,128)} %bitcast.6, s32[1,16]{1,0:T(1,128)} %bitcast.7, bf16[256,512]{1,0:T(8,128)(2,1)} %feat_ref.1, bf16[256,512]{1,0:T(8,128)(2,1)} %cot_any.1, bf16[512,512]{1,0:T(8,128)(2,1)} %w_any.1, ...), custom_call_target="tpu_custom_call" | custom-call | tf_op jit(solution)/shard_map/pallas_call | solution.py:620
  91.2 2.3 %shard_map.95 = (bf16[256,512]{1,0:T(8,128)(2,1)}, bf16[256,512]{1,0:T(8,128)(2,1)}, f32[512,512]{1,0:T(8,128)}) custom-call(bf16[256,512]{1,0:T(8,128)(2,1)} %get-tuple-element.6.act_in, bf16[512,256]{1,0:T(8,128)(2,1)} %get-tuple-element.7.grad_in, bf16[512,512]{1,0:T(8,128)(2,1)} %get-tuple-element.8.weight_in), custom_call_target="tpu_custom_call" | custom-call | tf_op jit(solution)/shard_map/pallas_call | solution.py:633
